TPU v7x, 32 devices: a whole 2x2x4 slice. The times are simulated.
32 devices in a mesh: areal: 8 (over z, y), layer: 4 (over x, core).
Axes of the slice: x: 2, y: 2, z: 4, core: 2. Of those that a mesh axis runs over, the one named last changes fastest.
Arguments:
- right_side: float32 [3, 16, 64, 256], P(None, 'layer', 'areal'), may hold values from -6 to 6
- diag_blocks: bfloat16 [3, 3, 16, 64, 256], P(None, None, 'layer', 'areal'), may hold values from -3 to 9
- couplings: bfloat16 [6, 3, 3, 16, 64, 256], P(None, None, None, 'layer', 'areal'), may hold values from -1 to 1
- pivot_inverse: bfloat16 [3, 3, 16, 64, 256], P(None, None, 'layer', 'areal'), may hold values from -0.2 to 0.2
- lower_blocks: bfloat16 [3, 3, 16, 64, 256], P(None, None, 'layer', 'areal'), may hold values from -0.1 to 1
- upper_blocks: bfloat16 [3, 3, 16, 64, 256], P(None, None, 'layer', 'areal'), may hold values from -0.1 to 1
- active_cells: int32 [16, 64, 256], P('layer', 'areal'), may hold values 0 or 1
- link_from: int32 [4, 32768], P('layer', 'areal'), may hold values from 0 to 8191
- link_owner: int32 [4, 32768, 1], P('layer', 'areal'), may hold values from 0 to 7; in each aligned block of 4096 rows (0 to 4095, 4096 to 8191, ..., all dimensions but the last counted through in order) at most 1024 rows name the same one
- link_target: int32 [4, 32768], P('layer', 'areal'), may hold values from 0 to 8191
- link_blocks: bfloat16 [3, 3, 4, 32768], P(None, None, 'layer', 'areal'), may hold values from -1.5 to 1.5
Outputs:
- update: float32 [3, 16, 64, 256], P(None, 'layer', 'areal')
- hessenberg: float32 [5, 4], replicated
Inputs may be any that keep to these rules, and one draw needn't show every extreme that they name: `link_owner`: among the 4096 connections listed on one device, at most 1024 name the same owner, and in every draw that number is reached.
All inputs are finite; a program needn't handle non-finite values. No bound on the sum of `active_cells` on one device may be relied on, other than what follows from the above.
Results may differ from a plain program's by a relative error of at most 0.0003.
Values sent between devices are 32-bit elements; how exact they have to be, the bound alone decides.
No kernel may reach another device: no remote copies, remote signals or barrier semaphores. Data moves between devices by JAX's collectives and lax.ppermute only.
A program may use at most 64 MiB of HBM per device.

v0:
```python
import jax
import jax.numpy as jnp
from jax import lax
from jax.sharding import PartitionSpec as P

ITERS = 4
SWEEP_BLOCKS = 2
tiny_square = 1e-06


def passed_along(array, axis, by):
    size = lax.axis_size(axis)
    pairs = [(i, i + by) for i in range(size) if 0 <= i + by < size]
    return lax.ppermute(array, axis, pairs)


def extended(block, sides, width):
    for axis, dim in sides:
        count = lax.axis_size(axis)
        forward = [(i, i + 1) for i in range(count - 1)]
        backward = [(target, source) for source, target in forward]
        low = lax.ppermute(
            lax.slice_in_dim(block, block.shape[dim] - width, None, axis=dim), axis, forward
        )
        high = lax.ppermute(lax.slice_in_dim(block, 0, width, axis=dim), axis, backward)
        block = jnp.concatenate([low, block, high], axis=dim)
    return block


def apply_block(matrix_blocks, vector):
    return jnp.sum(matrix_blocks.astype(jnp.float32) * vector[None], axis=1)


def sweep(values, blocks, downward, incoming):
    layers = values.shape[1]
    ordering = range(layers) if downward else range(layers - 1, -1, -1)
    previous = incoming
    results = [None] * layers
    for layer_at in ordering:
        previous = values[:, layer_at] - apply_block(blocks[:, :, layer_at], previous)
        results[layer_at] = previous
    return jnp.stack(results, axis=1)


def relay_sweep(values, blocks, downward):
    sections = lax.axis_size("layer")
    layer_index = lax.axis_index("layer")
    position = layer_index if downward else sections - 1 - layer_index
    block_rows = values.shape[2] // SWEEP_BLOCKS
    zero_edge = jnp.zeros((3, block_rows, values.shape[3]), jnp.float32)

    def moment(counter, state_pair):
        gathered, incoming = state_pair
        block_at = counter - position
        inside = jnp.logical_and(block_at >= 0, block_at < SWEEP_BLOCKS)
        first_row = jnp.clip(block_at, 0, SWEEP_BLOCKS - 1) * block_rows
        portion = lax.dynamic_slice_in_dim(values, first_row, block_rows, 2)
        coeffs = lax.dynamic_slice_in_dim(blocks, first_row, block_rows, 3)
        solved = sweep(portion, coeffs, downward, incoming)
        gathered = jnp.where(
            inside, lax.dynamic_update_slice_in_dim(gathered, solved, first_row, 2), gathered
        )
        if downward:
            passed = passed_along(solved[:, -1], "layer", 1)
        else:
            passed = passed_along(solved[:, 0], "layer", -1)
        return (gathered, passed)

    final_pair = lax.fori_loop(
        0, sections + SWEEP_BLOCKS - 1, moment, (jnp.zeros_like(values), zero_edge)
    )
    return final_pair[0]


def least_squares(hessenberg, initial):
    columns = hessenberg.shape[1]
    upper_form = hessenberg
    target_vector = jnp.zeros((columns + 1,), jnp.float32).at[0].set(initial)
    cosines = []
    sine_values = []
    for column in range(columns):
        entries = upper_form[:, column]
        for previous in range(column):
            upper_entry = entries[previous]
            lower_entry = entries[previous + 1]
            entries = entries.at[previous].set(
                cosines[previous] * upper_entry + sine_values[previous] * lower_entry
            )
            entries = entries.at[previous + 1].set(
                -sine_values[previous] * upper_entry + cosines[previous] * lower_entry
            )
        upper_entry = entries[column]
        lower_entry = entries[column + 1]
        radius = jnp.sqrt(upper_entry * upper_entry + lower_entry * lower_entry)
        cosines.append(upper_entry / radius)
        sine_values.append(lower_entry / radius)
        entries = entries.at[column].set(radius).at[column + 1].set(0.0)
        upper_form = upper_form.at[:, column].set(entries)
        leading = target_vector[column]
        target_vector = (
            target_vector.at[column]
            .set(cosines[column] * leading)
            .at[column + 1]
            .set(-sine_values[column] * leading)
        )
    solution = [None] * columns
    for row_at in range(columns - 1, -1, -1):
        partial_sum = target_vector[row_at]
        for later_row in range(row_at + 1, columns):
            partial_sum = partial_sum - upper_form[row_at, later_row] * solution[later_row]
        solution[row_at] = partial_sum / upper_form[row_at, row_at]
    return solution


def local(
    right_side,
    diag_blocks,
    couplings,
    pivot_inverse,
    lower_blocks,
    upper_blocks,
    active_cells,
    link_from,
    link_owner,
    link_target,
    link_blocks,
):
    active = active_cells.astype(jnp.float32)
    areal_count = lax.axis_size("areal")
    capacity = 2 * link_from.shape[1] // areal_count
    total_slots = capacity * areal_count
    owners = link_owner[0, :, 0]
    choose = (owners[:, None] == jnp.arange(areal_count, dtype=jnp.int32)[None, :]).astype(
        jnp.int32
    )
    before = jnp.sum((jnp.cumsum(choose, axis=0) - choose) * choose, axis=1)
    slot_of = owners * capacity + before
    outgoing_targets = jnp.zeros((1, total_slots), jnp.int32).at[0, slot_of].set(link_target[0])
    targets = lax.all_to_all(outgoing_targets, "areal", split_axis=1, concat_axis=1, tiled=True)[0]
    sources = link_from[0]
    link_matrix = link_blocks[:, :, 0]
    initial = jnp.sqrt(lax.psum(jnp.sum(right_side * right_side), ("areal", "layer")) + tiny_square)
    basis_list = [right_side / initial]
    directions = []
    hessenberg = jnp.zeros((ITERS + 1, ITERS), jnp.float32)
    for column in range(ITERS):
        scaled = apply_block(pivot_inverse, basis_list[column])
        forward = relay_sweep(scaled, lower_blocks, True)
        direction = relay_sweep(forward, upper_blocks, False)
        directions.append(direction)
        held_cells = direction * active[None]
        padded = extended(held_cells, (("areal", 2), ("layer", 1)), 1)
        padded = jnp.pad(padded, ((0, 0), (0, 0), (0, 0), (1, 1)))
        beside = [
            padded[:, :-2, 1:-1, 1:-1],
            padded[:, 2:, 1:-1, 1:-1],
            padded[:, 1:-1, :-2, 1:-1],
            padded[:, 1:-1, 2:, 1:-1],
            padded[:, 1:-1, 1:-1, :-2],
            padded[:, 1:-1, 1:-1, 2:],
        ]
        flattened = held_cells.reshape(3, -1)
        sending = apply_block(link_matrix, flattened[:, sources])
        outgoing = jnp.zeros((3, total_slots), jnp.float32).at[:, slot_of].set(sending)
        arriving = lax.all_to_all(outgoing, "areal", split_axis=1, concat_axis=1, tiled=True)
        result = apply_block(diag_blocks, held_cells)
        for operate_direction in range(6):
            result = result + apply_block(couplings[operate_direction], beside[operate_direction])
        result = result.reshape(3, -1).at[:, targets].add(arriving).reshape(direction.shape)
        result = active[None] * result + (1.0 - active[None]) * direction
        local_weights = jnp.stack([jnp.sum(earlier * result) for earlier in basis_list])
        weights, own_square = lax.psum(
            (local_weights, jnp.sum(result * result)), ("areal", "layer")
        )
        for position in range(column + 1):
            result = result - weights[position] * basis_list[position]
        length = jnp.sqrt(jnp.maximum(own_square - jnp.sum(weights * weights), 0.0) + tiny_square)
        hessenberg = (
            hessenberg.at[: column + 1, column].set(weights).at[column + 1, column].set(length)
        )
        basis_list.append(result / length)
    coefficients = least_squares(hessenberg, initial)
    update = coefficients[0] * directions[0]
    for position in range(1, ITERS):
        update = update + coefficients[position] * directions[position]
    return (update, hessenberg)


def solution(mesh):
    placed = (
        P(None, "layer", "areal", None),
        P(None, None, "layer", "areal", None),
        P(None, None, None, "layer", "areal", None),
        P(None, None, "layer", "areal", None),
        P(None, None, "layer", "areal", None),
        P(None, None, "layer", "areal", None),
        P("layer", "areal", None),
        P("layer", "areal"),
        P("layer", "areal", None),
        P("layer", "areal"),
        P(None, None, "layer", "areal"),
    )
    return jax.shard_map(
        local,
        mesh=mesh,
        in_specs=placed,
        out_specs=(P(None, "layer", "areal", None), P()),
        check_vma=False,
    )
```

profile of v0, /device:TPU:0, one launch (start us, length us, event | category | flops | bytes accessed | tf_op | source)
XLA Modules:
  0.0 1025.3 jit_solution(16016066879933783754)
XLA Ops:
  2.3 42.2 %psum.63 = f32[]{:T(128)} all-reduce(f32[]{:T(128)} %multiply_reduce_fusion.14), channel_id=1, replica_groups=mesh['areal'=8,'layer'=4] {'areal','layer'}, use_global_device_ids=true, to_apply=%region_1.2 | all-reduce | flops 1 | bytes 8 | tf_op jit(solution)/shard_map/psum | solution.py:142
  47.9 39.3 %while.161 = (s32[]{:T(128)}, f32[3,4,8,256]{3,2,1,0:T(8,128)S(1)}, f32[3,4,256]{2,1,0:T(4,128)S(1)}, s32[]{:T(128)}, f32[3,4,8,256]{3,2,1,0:T(8,128)S(1)}, /*in...) while((s32[]{:T(128)}, f32[3,4,8,256]{3,2,1,0:T(8,128)S(1)}, ...), condition=%wide.region_8.9_spmd, body=%wide.region_3.8_spmd.sunk | while | flops 172047 | bytes 665472 | solution.py:69
  87.3 26.6 %while.162 = (s32[]{:T(128)}, f32[3,4,8,256]{3,2,1,0:T(8,128)S(1)}, f32[3,4,256]{2,1,0:T(4,128)S(1)}, s32[]{:T(128)}, f32[3,4,8,256]{3,2,1,0:T(8,128)S(1)}, /*in...) while((s32[]{:T(128)}, f32[3,4,8,256]{3,2,1,0:T(8,128)S(1)}, ...), condition=%wide.region_14.15_spmd, body=%wide.region_9.14_spmd.sunk | while | flops 172047 | bytes 665472 | solution.py:69
  121.4 16.3 %scatter_custom_fusion.8 = s32[8192]{0:T(1024)} fusion(s32[4096]{0:T(1024)S(1)} %broadcast_select_fusion, s32[4096]{0:T(1024)} %bitcast.782, s32[]{:T(128)} %constant.1186.clone.1), kind=kCustom, calls=%fused_computation.380 | custom fusion | bytes 33280
  146.7 16.3 %gather_fusion = f32[4096,3]{1,0:T(8,128)} fusion(f32[3,8192]{0,1:T(8,128)} %bitcast.749, s32[4096]{0:T(1024)S(1)} %broadcast_clamp_fusion), kind=kCustom, calls=%fused_computation | custom fusion | bytes 114688 | tf_op jit(solution)/shard_map/gather | solution.py:163
  176.1 13.1 %scatter_custom_fusion = f32[3,8192]{0,1:T(8,128)} fusion(s32[4096]{0:T(1024)S(1)} %bitcast.771, f32[4096,3]{1,0:T(8,128)} %copy.146, f32[]{:T(128)} %constant.1184.clone.1), kind=kCustom, calls=%fused_computation.195 | custom fusion | bytes 98816 | tf_op jit(solution)/shard_map/scatter | solution.py:164
  214.0 56.3 %scatter_fusion = f32[3,8192]{0,1:T(8,128)} fusion(f32[3,8192]{0,1:T(8,128)} %bitcast.737, s32[8192]{0:T(1024)S(1)} %bitcast.757, f32[8192,3]{1,0:T(8,128)} %copy.148), kind=kCustom, calls=%fused_computation.5 | custom fusion | flops 24576 | bytes 327680 | tf_op jit(solution)/shard_map/scatter-add | solution.py:169
  273.8 40.0 %all-reduce.9 = (f32[]{:T(128)}, f32[1]{0:T(128)}) all-reduce(f32[]{:T(128)} %get-tuple-element.1555, f32[1]{0:T(128)} %bitcast.155), channel_id=1, replica_groups=mesh['areal'=8,'layer'=4] {'areal','layer'}, use_global_device_ids=true, to_apply=%region_32.33 | all-reduce | flops 2 | bytes 16 | tf_op jit(solution)/shard_map/psum | solution.py:172
  316.6 24.0 %while.163 = (s32[]{:T(128)}, f32[3,4,8,256]{3,2,1,0:T(8,128)S(1)}, f32[3,4,256]{2,1,0:T(4,128)S(1)}, s32[]{:T(128)}, f32[3,4,8,256]{3,2,1,0:T(8,128)S(1)}, /*in...) while((s32[]{:T(128)}, f32[3,4,8,256]{3,2,1,0:T(8,128)S(1)}, ...), condition=%wide.region_40.41_spmd, body=%wide.region_35.40_spmd.sunk | while | flops 172047 | bytes 665472 | solution.py:69
  340.6 26.6 %while.164 = (s32[]{:T(128)}, f32[3,4,8,256]{3,2,1,0:T(8,128)S(1)}, f32[3,4,256]{2,1,0:T(4,128)S(1)}, s32[]{:T(128)}, f32[3,4,8,256]{3,2,1,0:T(8,128)S(1)}, /*in...) while((s32[]{:T(128)}, f32[3,4,8,256]{3,2,1,0:T(8,128)S(1)}, ...), condition=%wide.region_46.47_spmd, body=%wide.region_41.46_spmd.sunk | while | flops 172047 | bytes 665472 | solution.py:69
  374.2 16.3 %gather_fusion.1 = f32[4096,3]{1,0:T(8,128)} fusion(f32[3,8192]{0,1:T(8,128)} %bitcast.752, s32[4096]{0:T(1024)S(1)} %broadcast_clamp_fusion), kind=kCustom, calls=%fused_computation.1 | custom fusion | bytes 114688 | tf_op jit(solution)/shard_map/gather | solution.py:163
  400.2 13.1 %scatter_custom_fusion.2 = f32[3,8192]{0,1:T(8,128)} fusion(s32[4096]{0:T(1024)S(1)} %bitcast.772, f32[4096,3]{1,0:T(8,128)} %copy.155, f32[]{:T(128)} %constant.1184.clone.1), kind=kCustom, calls=%fused_computation.193 | custom fusion | bytes 98816 | tf_op jit(solution)/shard_map/scatter | solution.py:164
  433.6 55.8 %scatter_fusion.1 = f32[3,8192]{0,1:T(8,128)} fusion(f32[3,8192]{0,1:T(8,128)} %bitcast.741, s32[8192]{0:T(1024)S(1)} %bitcast.758, f32[8192,3]{1,0:T(8,128)} %copy.157), kind=kCustom, calls=%fused_computation.7 | custom fusion | flops 24576 | bytes 327680 | tf_op jit(solution)/shard_map/scatter-add | solution.py:169
  494.3 39.7 %all-reduce.8 = (f32[]{:T(128)}, f32[2]{0:T(128)S(1)}) all-reduce(f32[]{:T(128)} %get-tuple-element.1552, f32[2]{0:T(128)S(1)} %pad_maximum_fusion.44), channel_id=1, replica_groups=mesh['areal'=8,'layer'=4] {'areal','layer'}, use_global_device_ids=true, to_apply=%region_61.62 | all-reduce | flops 3 | bytes 24 | tf_op jit(solution)/shard_map/psum | solution.py:172
  538.0 24.0 %while.165 = (s32[]{:T(128)}, f32[3,4,8,256]{3,2,1,0:T(8,128)S(1)}, f32[3,4,256]{2,1,0:T(4,128)S(1)}, s32[]{:T(128)}, f32[3,4,8,256]{3,2,1,0:T(8,128)S(1)}, /*in...) while((s32[]{:T(128)}, f32[3,4,8,256]{3,2,1,0:T(8,128)S(1)}, ...), condition=%wide.region_70.71_spmd, body=%wide.region_65.70_spmd.sunk | while | flops 172047 | bytes 665472 | solution.py:69
  562.1 26.6 %while.166 = (s32[]{:T(128)}, f32[3,4,8,256]{3,2,1,0:T(8,128)S(1)}, f32[3,4,256]{2,1,0:T(4,128)S(1)}, s32[]{:T(128)}, f32[3,4,8,256]{3,2,1,0:T(8,128)S(1)}, /*in...) while((s32[]{:T(128)}, f32[3,4,8,256]{3,2,1,0:T(8,128)S(1)}, ...), condition=%wide.region_76.77_spmd, body=%wide.region_71.0_spmd.sunk | while | flops 172047 | bytes 665472 | solution.py:69
  591.3 16.3 %gather_fusion.2 = f32[4096,3]{1,0:T(8,128)} fusion(f32[3,8192]{0,1:T(8,128)} %bitcast.751, s32[4096]{0:T(1024)S(1)} %broadcast_clamp_fusion), kind=kCustom, calls=%fused_computation.2 | custom fusion | bytes 114688 | tf_op jit(solution)/shard_map/gather | solution.py:163
  653.2 55.8 %scatter_fusion.2 = f32[3,8192]{0,1:T(8,128)} fusion(f32[3,8192]{0,1:T(8,128)} %bitcast.743, s32[8192]{0:T(1024)S(1)} %bitcast.759, f32[8192,3]{1,0:T(8,128)} %copy.166), kind=kCustom, calls=%fused_computation.9 | custom fusion | flops 24576 | bytes 327680 | tf_op jit(solution)/shard_map/scatter-add | solution.py:169
  714.5 44.2 %all-reduce.7 = (f32[]{:T(128)}, f32[3]{0:T(128)S(1)}) all-reduce(f32[]{:T(128)} %get-tuple-element.1548, f32[3]{0:T(128)S(1)} %pad_maximum_fusion.45), channel_id=1, replica_groups=mesh['areal'=8,'layer'=4] {'areal','layer'}, use_global_device_ids=true, to_apply=%region_92.93 | all-reduce | flops 4 | bytes 32 | tf_op jit(solution)/shard_map/psum | solution.py:172
  763.3 24.0 %while.167 = (s32[]{:T(128)}, f32[3,4,8,256]{3,2,1,0:T(8,128)S(1)}, f32[3,4,256]{2,1,0:T(4,128)S(1)}, s32[]{:T(128)}, f32[3,4,8,256]{3,2,1,0:T(8,128)S(1)}, /*in...) while((s32[]{:T(128)}, f32[3,4,8,256]{3,2,1,0:T(8,128)S(1)}, ...), condition=%wide.region_101.102_spmd, body=%wide.region_96.101_spmd.sunk | while | flops 172047 | bytes 665472 | solution.py:69
  787.3 26.6 %while.168 = (s32[]{:T(128)}, f32[3,4,8,256]{3,2,1,0:T(8,128)S(1)}, f32[3,4,256]{2,1,0:T(4,128)S(1)}, s32[]{:T(128)}, f32[3,4,8,256]{3,2,1,0:T(8,128)S(1)}, /*in...) while((s32[]{:T(128)}, f32[3,4,8,256]{3,2,1,0:T(8,128)S(1)}, ...), condition=%wide.region_107.108_spmd, body=%wide.region_102.0_spmd.sunk | while | flops 172047 | bytes 665472 | solution.py:69
  816.6 16.3 %gather_fusion.3 = f32[4096,3]{1,0:T(8,128)} fusion(f32[3,8192]{0,1:T(8,128)} %bitcast.750, s32[4096]{0:T(1024)S(1)} %broadcast_clamp_fusion), kind=kCustom, calls=%fused_computation.3 | custom fusion | bytes 114688 | tf_op jit(solution)/shard_map/gather | solution.py:163
  878.4 55.8 %scatter_fusion.3 = f32[3,8192]{0,1:T(8,128)} fusion(f32[3,8192]{0,1:T(8,128)} %bitcast.739, s32[8192]{0:T(1024)S(1)} %bitcast.760, f32[8192,3]{1,0:T(8,128)} %copy.175), kind=kCustom, calls=%fused_computation.11 | custom fusion | flops 24576 | bytes 327680 | tf_op jit(solution)/shard_map/scatter-add | solution.py:169
  940.4 43.9 %all-reduce.6 = (f32[4]{0:T(128)S(1)}, f32[]{:T(128)}) all-reduce(f32[4]{0:T(128)S(1)} %pad_maximum_fusion.46, f32[]{:T(128)} %get-tuple-element.1542), channel_id=1, replica_groups=mesh['areal'=8,'layer'=4] {'areal','layer'}, use_global_device_ids=true, to_apply=%region_122.123 | all-reduce | flops 5 | bytes 40 | tf_op jit(solution)/shard_map/psum | solution.py:172
  (731 shorter events, 446.6 us)
Async XLA Ops:
  56.6 5.7 collective-permute-start
  92.7 5.6 collective-permute-start.1
  114.0 54.0 %collective-permute-start.8 = (f32[3,4,1,256]{3,2,1,0:T(1,128)S(1)}, f32[3,4,1,256]{3,2,1,0:T(1,128)S(1)}, u32[]{:S(2)}, u32[]{:S(2)}) collective-permute-start(f32[3,4,1,256]{3,2,1,0:T(1,128)S(1)} %get-tuple-element.1733), channel_id=1, source_target_pairs={{0,4},{4,8},{8,12},{12,16},{16,20},{20,24},{24,28},{1,5},{5,9},{9,... | collective-permute-start | bytes 36872 | tf_op jit(solution)/shard_map/ppermute | solution.py:22
  116.7 51.2 %collective-permute-start.9 = (f32[3,4,1,256]{3,2,1,0:T(1,128)S(1)}, f32[3,4,1,256]{3,2,1,0:T(1,128)S(1)}, u32[]{:S(2)}, u32[]{:S(2)}) collective-permute-start(f32[3,4,1,256]{3,2,1,0:T(1,128)S(1)} %get-tuple-element.1734), channel_id=1, source_target_pairs={{4,0},{8,4},{12,8},{16,12},{20,16},{24,20},{28,24},{5,1},{9,5},{13... | collective-permute-start | bytes 36872 | tf_op jit(solution)/shard_map/ppermute | solution.py:25
  137.7 60.2 %all-to-all-start = ((s32[1,8,1024]{2,0,1:T(1,128)}), s32[1,8,1024]{2,0,1:T(1,128)S(1)}, u32[]{:S(2)}, u32[]{:S(2)}) async-start(s32[1,8,1024]{2,0,1:T(1,128)} %bitcast.141), calls=%async_computation | async-start | bytes 65536 | tf_op jit(solution)/shard_map/all_to_all | solution.py:139
  168.0 26.6 %collective-permute-start.10 = (f32[3,1,10,256]{3,2,1,0:T(8,128)S(1)}, f32[3,1,10,256]{3,2,1,0:T(8,128)S(1)}, u32[]{:S(2)}, u32[]{:S(2)}) collective-permute-start(f32[3,1,10,256]{3,2,1,0:T(8,128)S(1)} %get-tuple-element.1718), channel_id=1, source_target_pairs={{0,1},{1,2},{2,3},{4,5},{5,6},{6,7},{8,9},{9,10},{10,11},{12,13},{... | collective-permute-start | bytes 92168 | tf_op jit(solution)/shard_map/ppermute | solution.py:22
  171.5 23.1 %collective-permute-start.11 = (f32[3,1,10,256]{3,2,1,0:T(8,128)S(1)}, f32[3,1,10,256]{3,2,1,0:T(8,128)S(1)}, u32[]{:S(2)}, u32[]{:S(2)}) collective-permute-start(f32[3,1,10,256]{3,2,1,0:T(8,128)S(1)} %get-tuple-element.1717), channel_id=1, source_target_pairs={{1,0},{2,1},{3,2},{5,4},{6,5},{7,6},{9,8},{10,9},{11,10},{13,12},{... | collective-permute-start | bytes 92168 | tf_op jit(solution)/shard_map/ppermute | solution.py:25
  197.8 13.5 %all-to-all-start.1 = ((f32[3,8,1024]{2,0,1:T(4,128)}), f32[3,8,1024]{2,0,1:T(4,128)S(1)}, u32[]{:S(2)}, u32[]{:S(2)}) async-start(f32[3,8,1024]{2,0,1:T(4,128)} %copy.147), calls=%async_computation.1 | async-start | bytes 262144 | tf_op jit(solution)/shard_map/all_to_all | solution.py:165
  319.2 5.7 collective-permute-start.2
  367.2 25.4 %collective-permute-start.12 = (f32[3,4,1,256]{3,2,1,0:T(1,128)S(1)}, f32[3,4,1,256]{3,2,1,0:T(1,128)S(1)}, u32[]{:S(2)}, u32[]{:S(2)}) collective-permute-start(f32[3,4,1,256]{3,2,1,0:T(1,128)S(1)} %get-tuple-element.1731), channel_id=1, source_target_pairs={{0,4},{4,8},{8,12},{12,16},{16,20},{20,24},{24,28},{1,5},{5,9},{9,... | collective-permute-start | bytes 36872 | tf_op jit(solution)/shard_map/ppermute | solution.py:22
  370.3 22.4 %collective-permute-start.13 = (f32[3,4,1,256]{3,2,1,0:T(1,128)S(1)}, f32[3,4,1,256]{3,2,1,0:T(1,128)S(1)}, u32[]{:S(2)}, u32[]{:S(2)}) collective-permute-start(f32[3,4,1,256]{3,2,1,0:T(1,128)S(1)} %get-tuple-element.1732), channel_id=1, source_target_pairs={{4,0},{8,4},{12,8},{16,12},{20,16},{24,20},{28,24},{5,1},{9,5},{13... | collective-permute-start | bytes 36872 | tf_op jit(solution)/shard_map/ppermute | solution.py:25
  392.7 30.8 %collective-permute-start.14 = (f32[3,1,10,256]{3,2,1,0:T(8,128)S(1)}, f32[3,1,10,256]{3,2,1,0:T(8,128)S(1)}, u32[]{:S(2)}, u32[]{:S(2)}) collective-permute-start(f32[3,1,10,256]{3,2,1,0:T(8,128)S(1)} %get-tuple-element.1714), channel_id=1, source_target_pairs={{0,1},{1,2},{2,3},{4,5},{5,6},{6,7},{8,9},{9,10},{10,11},{12,13},{... | collective-permute-start | bytes 92168 | tf_op jit(solution)/shard_map/ppermute | solution.py:22
  396.8 26.8 %collective-permute-start.15 = (f32[3,1,10,256]{3,2,1,0:T(8,128)S(1)}, f32[3,1,10,256]{3,2,1,0:T(8,128)S(1)}, u32[]{:S(2)}, u32[]{:S(2)}) collective-permute-start(f32[3,1,10,256]{3,2,1,0:T(8,128)S(1)} %get-tuple-element.1713), channel_id=1, source_target_pairs={{1,0},{2,1},{3,2},{5,4},{6,5},{7,6},{9,8},{10,9},{11,10},{13,12},{... | collective-permute-start | bytes 92168 | tf_op jit(solution)/shard_map/ppermute | solution.py:25
  416.7 14.3 %all-to-all-start.2 = ((f32[3,8,1024]{2,0,1:T(4,128)}), f32[3,8,1024]{2,0,1:T(4,128)S(1)}, u32[]{:S(2)}, u32[]{:S(2)}) async-start(f32[3,8,1024]{2,0,1:T(4,128)} %copy.156), calls=%async_computation.2 | async-start | bytes 262144 | tf_op jit(solution)/shard_map/all_to_all | solution.py:165
  540.6 5.7 collective-permute-start.4
  609.8 29.0 %collective-permute-start.16 = (f32[3,4,1,256]{3,2,1,0:T(1,128)S(1)}, f32[3,4,1,256]{3,2,1,0:T(1,128)S(1)}, u32[]{:S(2)}, u32[]{:S(2)}) collective-permute-start(f32[3,4,1,256]{3,2,1,0:T(1,128)S(1)} %get-tuple-element.1729), channel_id=1, source_target_pairs={{0,4},{4,8},{8,12},{12,16},{16,20},{20,24},{24,28},{1,5},{5,9},{9,... | collective-permute-start | bytes 36872 | tf_op jit(solution)/shard_map/ppermute | solution.py:22
  612.2 26.7 %collective-permute-start.17 = (f32[3,4,1,256]{3,2,1,0:T(1,128)S(1)}, f32[3,4,1,256]{3,2,1,0:T(1,128)S(1)}, u32[]{:S(2)}, u32[]{:S(2)}) collective-permute-start(f32[3,4,1,256]{3,2,1,0:T(1,128)S(1)} %get-tuple-element.1730), channel_id=1, source_target_pairs={{4,0},{8,4},{12,8},{16,12},{20,16},{24,20},{28,24},{5,1},{9,5},{13... | collective-permute-start | bytes 36872 | tf_op jit(solution)/shard_map/ppermute | solution.py:25
  632.1 18.4 %all-to-all-start.3 = ((f32[3,8,1024]{2,0,1:T(4,128)}), f32[3,8,1024]{2,0,1:T(4,128)S(1)}, u32[]{:S(2)}, u32[]{:S(2)}) async-start(f32[3,8,1024]{2,0,1:T(4,128)} %copy.165), calls=%async_computation.3 | async-start | bytes 262144 | tf_op jit(solution)/shard_map/all_to_all | solution.py:165
  638.9 8.3 collective-permute-start.18
  765.9 5.7 collective-permute-start.6
  835.1 29.0 %collective-permute-start.20 = (f32[3,4,1,256]{3,2,1,0:T(1,128)S(1)}, f32[3,4,1,256]{3,2,1,0:T(1,128)S(1)}, u32[]{:S(2)}, u32[]{:S(2)}) collective-permute-start(f32[3,4,1,256]{3,2,1,0:T(1,128)S(1)} %get-tuple-element.1727), channel_id=1, source_target_pairs={{0,4},{4,8},{8,12},{12,16},{16,20},{20,24},{24,28},{1,5},{5,9},{9,... | collective-permute-start | bytes 36872 | tf_op jit(solution)/shard_map/ppermute | solution.py:22
  837.2 26.8 %collective-permute-start.21 = (f32[3,4,1,256]{3,2,1,0:T(1,128)S(1)}, f32[3,4,1,256]{3,2,1,0:T(1,128)S(1)}, u32[]{:S(2)}, u32[]{:S(2)}) collective-permute-start(f32[3,4,1,256]{3,2,1,0:T(1,128)S(1)} %get-tuple-element.1728), channel_id=1, source_target_pairs={{4,0},{8,4},{12,8},{16,12},{20,16},{24,20},{28,24},{5,1},{9,5},{13... | collective-permute-start | bytes 36872 | tf_op jit(solution)/shard_map/ppermute | solution.py:25
  857.2 18.6 %all-to-all-start.4 = ((f32[3,8,1024]{2,0,1:T(4,128)}), f32[3,8,1024]{2,0,1:T(4,128)S(1)}, u32[]{:S(2)}, u32[]{:S(2)}) async-start(f32[3,8,1024]{2,0,1:T(4,128)} %copy.174), calls=%async_computation.4 | async-start | bytes 262144 | tf_op jit(solution)/shard_map/all_to_all | solution.py:165
  864.1 8.3 collective-permute-start.22
  (52 other events, 1162.2 us)
where the time goes:
time: 1040 us; the launch traced here: 1030 us
  other arithmetic  286 us (28%)
  local copies, waits for them, and re-layouts  223 us (21%)
  blocking collectives  210 us (20%)
  starting transfers between devices  168 us (16%)
  waiting for transfers between devices  101 us (10%)
  between operations  34.5 us (3%)
    scatter-add x4, other arithmetic, local(): result.reshape(3, -1).at[:, targets].add(arriving).reshape(direction.shape)  224 us
    psum x4, blocking collectives, local(): lax.psum((local_weights, jnp.sum(result * result)), ('areal', 'layer'))  168 us
    ppermute x40, starting transfers between devices, passed_along(): return lax.ppermute(array, axis, pairs)  101 us
    ppermute x40, waiting for transfers between devices, passed_along(): return lax.ppermute(array, axis, pairs)  88.8 us
    gather x8, local copies, waits for them, and re-layouts, local(): sending = apply_block(link_matrix, flattened[:, sources])  73.9 us
    scatter x4, local copies, waits for them, and re-layouts, local(): jnp.zeros((3, total_slots), jnp.float32).at[:, slot_of].set(sending)  52.2 us
    psum x1, blocking collectives, local(): lax.psum(jnp.sum(right_side * right_side), ('areal', 'layer')) + tiny_square  42.2 us
    all_to_all x4, starting transfers between devices, local(): lax.all_to_all(outgoing, 'areal', split_axis=1, concat_axis=1, tiled=True)  25.3 us
  transfers between devices with their start and end apart: 61, of which 42 were waited for; matrix products, arithmetic and copies ran while one was open for 16% of the time, Pallas kernels for 0%

commit v1 on v0

--- a/solution.py
+++ b/solution.py
@@ -170,7 +170,7 @@
         result = active[None] * result + (1.0 - active[None]) * direction
         local_weights = jnp.stack([jnp.sum(earlier * result) for earlier in basis_list])
         weights, own_square = lax.psum(
-            (local_weights, jnp.sum(result * result)), ("areal", "layer")
+            lax.psum((local_weights, jnp.sum(result * result)), "layer"), "areal"
         )
         for position in range(column + 1):
             result = result - weights[position] * basis_list[position]

time: 1040 us -> 977 us (0.939)
  blocking collectives: 210 us -> 159 us
    psum x4 -> x8, blocking collectives: 168 us -> 117 us  [the longest x4 85.5 us: local(): lax.psum(lax.psum((local_weights, jnp.sum(result * result)), 'layer'), 'a...]
  transfers between devices with their start and end apart: 61 -> 61, of which waited for: 42 -> 42; matrix products, arithmetic and copies ran while one was open for 16% -> 17% of each run, Pallas kernels for 0% -> 0%
where the time goes in v1:
time: 977 us; the launch traced here: 964 us
  other arithmetic  286 us (29%)
  local copies, waits for them, and re-layouts  223 us (23%)
  blocking collectives  159 us (16%)
  starting transfers between devices  158 us (16%)
  waiting for transfers between devices  101 us (10%)
  between operations  34.4 us (4%)
    scatter-add x4, other arithmetic, local(): result.reshape(3, -1).at[:, targets].add(arriving).reshape(direction.shape)  223 us
    ppermute x40, starting transfers between devices, passed_along(): return lax.ppermute(array, axis, pairs)  101 us
    ppermute x40, waiting for transfers between devices, passed_along(): return lax.ppermute(array, axis, pairs)  88.8 us
    psum x4, blocking collectives, local(): lax.psum(lax.psum((local_weights, jnp.sum(result * result)), 'layer'), 'a...  85.5 us
    gather x8, local copies, waits for them, and re-layouts, local(): sending = apply_block(link_matrix, flattened[:, sources])  73.9 us
    scatter x4, local copies, waits for them, and re-layouts, local(): jnp.zeros((3, total_slots), jnp.float32).at[:, slot_of].set(sending)  52.4 us
    psum x1, blocking collectives, local(): lax.psum(jnp.sum(right_side * right_side), ('areal', 'layer')) + tiny_square  42.2 us
    psum x4, blocking collectives, local(): lax.psum((local_weights, jnp.sum(result * result)), 'layer')  31.3 us
  transfers between devices with their start and end apart: 61, of which 42 were waited for; matrix products, arithmetic and copies ran while one was open for 17% of the time, Pallas kernels for 0%

profile of v1, /device:TPU:0, one launch (start us, length us, event | category | flops | bytes accessed | tf_op | source)
XLA Modules:
  0.0 963.9 jit_solution(878828919884726091)
XLA Ops:
  2.3 42.2 %psum.119 = f32[]{:T(128)} all-reduce(f32[]{:T(128)} %multiply_reduce_fusion.14), channel_id=1, replica_groups=mesh['areal'=8,'layer'=4] {'areal','layer'}, use_global_device_ids=true, to_apply=%region_1.2 | all-reduce | flops 1 | bytes 8 | tf_op jit(solution)/shard_map/psum | solution.py:142
  47.9 39.3 %while.161 = (s32[]{:T(128)}, f32[3,4,8,256]{3,2,1,0:T(8,128)S(1)}, f32[3,4,256]{2,1,0:T(4,128)S(1)}, s32[]{:T(128)}, f32[3,4,8,256]{3,2,1,0:T(8,128)S(1)}, /*in...) while((s32[]{:T(128)}, f32[3,4,8,256]{3,2,1,0:T(8,128)S(1)}, ...), condition=%wide.region_8.9_spmd, body=%wide.region_3.8_spmd.sunk | while | flops 172047 | bytes 665472 | solution.py:69
  87.3 26.6 %while.162 = (s32[]{:T(128)}, f32[3,4,8,256]{3,2,1,0:T(8,128)S(1)}, f32[3,4,256]{2,1,0:T(4,128)S(1)}, s32[]{:T(128)}, f32[3,4,8,256]{3,2,1,0:T(8,128)S(1)}, /*in...) while((s32[]{:T(128)}, f32[3,4,8,256]{3,2,1,0:T(8,128)S(1)}, ...), condition=%wide.region_14.15_spmd, body=%wide.region_9.14_spmd.sunk | while | flops 172047 | bytes 665472 | solution.py:69
  121.4 16.3 %scatter_custom_fusion.8 = s32[8192]{0:T(1024)} fusion(s32[4096]{0:T(1024)S(1)} %broadcast_select_fusion, s32[4096]{0:T(1024)} %bitcast.782, s32[]{:T(128)} %constant.1186.clone.1), kind=kCustom, calls=%fused_computation.380 | custom fusion | bytes 33280
  146.7 16.3 %gather_fusion = f32[4096,3]{1,0:T(8,128)} fusion(f32[3,8192]{0,1:T(8,128)} %bitcast.749, s32[4096]{0:T(1024)S(1)} %broadcast_clamp_fusion), kind=kCustom, calls=%fused_computation | custom fusion | bytes 114688 | tf_op jit(solution)/shard_map/gather | solution.py:163
  176.1 13.1 %scatter_custom_fusion = f32[3,8192]{0,1:T(8,128)} fusion(s32[4096]{0:T(1024)S(1)} %bitcast.771, f32[4096,3]{1,0:T(8,128)} %copy.146, f32[]{:T(128)} %constant.1184.clone.1), kind=kCustom, calls=%fused_computation.195 | custom fusion | bytes 98816 | tf_op jit(solution)/shard_map/scatter | solution.py:164
  213.9 55.9 %scatter_fusion = f32[3,8192]{0,1:T(8,128)} fusion(f32[3,8192]{0,1:T(8,128)} %bitcast.737, s32[8192]{0:T(1024)S(1)} %bitcast.757, f32[8192,3]{1,0:T(8,128)} %copy.148), kind=kCustom, calls=%fused_computation.5 | custom fusion | flops 24576 | bytes 327680 | tf_op jit(solution)/shard_map/scatter-add | solution.py:169
  281.7 19.5 %all-reduce.9 = (f32[]{:T(128)}, f32[1]{0:T(128)}) all-reduce(f32[]{:T(128)} %get-tuple-element.1666, f32[1]{0:T(128)} %get-tuple-element.1667), channel_id=1, replica_groups=mesh['areal'=8,'layer'=4] {'areal'}, use_global_device_ids=true, to_apply=%region_34.35 | all-reduce | flops 2 | bytes 16 | tf_op jit(solution)/shard_map/psum | solution.py:172
  303.9 23.9 %while.163 = (s32[]{:T(128)}, f32[3,4,8,256]{3,2,1,0:T(8,128)S(1)}, f32[3,4,256]{2,1,0:T(4,128)S(1)}, s32[]{:T(128)}, f32[3,4,8,256]{3,2,1,0:T(8,128)S(1)}, /*in...) while((s32[]{:T(128)}, f32[3,4,8,256]{3,2,1,0:T(8,128)S(1)}, ...), condition=%wide.region_42.43_spmd, body=%wide.region_37.42_spmd.sunk | while | flops 172047 | bytes 665472 | solution.py:69
  327.8 26.6 %while.164 = (s32[]{:T(128)}, f32[3,4,8,256]{3,2,1,0:T(8,128)S(1)}, f32[3,4,256]{2,1,0:T(4,128)S(1)}, s32[]{:T(128)}, f32[3,4,8,256]{3,2,1,0:T(8,128)S(1)}, /*in...) while((s32[]{:T(128)}, f32[3,4,8,256]{3,2,1,0:T(8,128)S(1)}, ...), condition=%wide.region_48.49_spmd, body=%wide.region_43.48_spmd.sunk | while | flops 172047 | bytes 665472 | solution.py:69
  360.6 16.3 %gather_fusion.1 = f32[4096,3]{1,0:T(8,128)} fusion(f32[3,8192]{0,1:T(8,128)} %bitcast.752, s32[4096]{0:T(1024)S(1)} %broadcast_clamp_fusion), kind=kCustom, calls=%fused_computation.1 | custom fusion | bytes 114688 | tf_op jit(solution)/shard_map/gather | solution.py:163
  417.7 55.8 %scatter_fusion.1 = f32[3,8192]{0,1:T(8,128)} fusion(f32[3,8192]{0,1:T(8,128)} %bitcast.741, s32[8192]{0:T(1024)S(1)} %bitcast.758, f32[8192,3]{1,0:T(8,128)} %copy.157), kind=kCustom, calls=%fused_computation.7 | custom fusion | flops 24576 | bytes 327680 | tf_op jit(solution)/shard_map/scatter-add | solution.py:169
  485.2 19.9 %all-reduce.8 = (f32[]{:T(128)}, f32[2]{0:T(128)S(1)}) all-reduce(f32[]{:T(128)} %get-tuple-element.1664, f32[2]{0:T(128)S(1)} %get-tuple-element.1665), channel_id=1, replica_groups=mesh['areal'=8,'layer'=4] {'areal'}, use_global_device_ids=true, to_apply=%region_65.66 | all-reduce | flops 3 | bytes 24 | tf_op jit(solution)/shard_map/psum | solution.py:172
  509.0 23.9 %while.165 = (s32[]{:T(128)}, f32[3,4,8,256]{3,2,1,0:T(8,128)S(1)}, f32[3,4,256]{2,1,0:T(4,128)S(1)}, s32[]{:T(128)}, f32[3,4,8,256]{3,2,1,0:T(8,128)S(1)}, /*in...) while((s32[]{:T(128)}, f32[3,4,8,256]{3,2,1,0:T(8,128)S(1)}, ...), condition=%wide.region_74.75_spmd, body=%wide.region_69.74_spmd.sunk | while | flops 172047 | bytes 665472 | solution.py:69
  533.0 26.6 %while.166 = (s32[]{:T(128)}, f32[3,4,8,256]{3,2,1,0:T(8,128)S(1)}, f32[3,4,256]{2,1,0:T(4,128)S(1)}, s32[]{:T(128)}, f32[3,4,8,256]{3,2,1,0:T(8,128)S(1)}, /*in...) while((s32[]{:T(128)}, f32[3,4,8,256]{3,2,1,0:T(8,128)S(1)}, ...), condition=%wide.region_80.81_spmd, body=%wide.region_75.0_spmd.sunk | while | flops 172047 | bytes 665472 | solution.py:69
  562.3 16.3 %gather_fusion.2 = f32[4096,3]{1,0:T(8,128)} fusion(f32[3,8192]{0,1:T(8,128)} %bitcast.751, s32[4096]{0:T(1024)S(1)} %broadcast_clamp_fusion), kind=kCustom, calls=%fused_computation.2 | custom fusion | bytes 114688 | tf_op jit(solution)/shard_map/gather | solution.py:163
  620.9 55.8 %scatter_fusion.2 = f32[3,8192]{0,1:T(8,128)} fusion(f32[3,8192]{0,1:T(8,128)} %bitcast.743, s32[8192]{0:T(1024)S(1)} %bitcast.759, f32[8192,3]{1,0:T(8,128)} %copy.166), kind=kCustom, calls=%fused_computation.9 | custom fusion | flops 24576 | bytes 327680 | tf_op jit(solution)/shard_map/scatter-add | solution.py:169
  690.3 23.1 %all-reduce.7 = (f32[]{:T(128)}, f32[3]{0:T(128)S(1)}) all-reduce(f32[]{:T(128)} %get-tuple-element.1662, f32[3]{0:T(128)S(1)} %get-tuple-element.1663), channel_id=1, replica_groups=mesh['areal'=8,'layer'=4] {'areal'}, use_global_device_ids=true, to_apply=%region_98.99 | all-reduce | flops 4 | bytes 32 | tf_op jit(solution)/shard_map/psum | solution.py:172
  718.0 23.9 %while.167 = (s32[]{:T(128)}, f32[3,4,8,256]{3,2,1,0:T(8,128)S(1)}, f32[3,4,256]{2,1,0:T(4,128)S(1)}, s32[]{:T(128)}, f32[3,4,8,256]{3,2,1,0:T(8,128)S(1)}, /*in...) while((s32[]{:T(128)}, f32[3,4,8,256]{3,2,1,0:T(8,128)S(1)}, ...), condition=%wide.region_107.108_spmd, body=%wide.region_102.107_spmd.sunk | while | flops 172047 | bytes 665472 | solution.py:69
  742.0 26.6 %while.168 = (s32[]{:T(128)}, f32[3,4,8,256]{3,2,1,0:T(8,128)S(1)}, f32[3,4,256]{2,1,0:T(4,128)S(1)}, s32[]{:T(128)}, f32[3,4,8,256]{3,2,1,0:T(8,128)S(1)}, /*in...) while((s32[]{:T(128)}, f32[3,4,8,256]{3,2,1,0:T(8,128)S(1)}, ...), condition=%wide.region_113.114_spmd, body=%wide.region_108.0_spmd.sunk | while | flops 172047 | bytes 665472 | solution.py:69
  771.2 16.3 %gather_fusion.3 = f32[4096,3]{1,0:T(8,128)} fusion(f32[3,8192]{0,1:T(8,128)} %bitcast.750, s32[4096]{0:T(1024)S(1)} %broadcast_clamp_fusion), kind=kCustom, calls=%fused_computation.3 | custom fusion | bytes 114688 | tf_op jit(solution)/shard_map/gather | solution.py:163
  794.4 13.2 %scatter_custom_fusion.6 = f32[3,8192]{0,1:T(8,128)} fusion(s32[4096]{0:T(1024)S(1)} %bitcast.774, f32[4096,3]{1,0:T(8,128)} %copy.173, f32[]{:T(128)} %constant.1184.clone.1), kind=kCustom, calls=%fused_computation.189 | custom fusion | bytes 98816 | tf_op jit(solution)/shard_map/scatter | solution.py:164
  829.8 55.8 %scatter_fusion.3 = f32[3,8192]{0,1:T(8,128)} fusion(f32[3,8192]{0,1:T(8,128)} %bitcast.739, s32[8192]{0:T(1024)S(1)} %bitcast.760, f32[8192,3]{1,0:T(8,128)} %copy.175), kind=kCustom, calls=%fused_computation.11 | custom fusion | flops 24576 | bytes 327680 | tf_op jit(solution)/shard_map/scatter-add | solution.py:169
  899.8 23.1 %all-reduce.6 = (f32[4]{0:T(128)S(1)}, f32[]{:T(128)}) all-reduce(f32[4]{0:T(128)S(1)} %get-tuple-element.1660, f32[]{:T(128)} %get-tuple-element.1661), channel_id=1, replica_groups=mesh['areal'=8,'layer'=4] {'areal'}, use_global_device_ids=true, to_apply=%region_129.130 | all-reduce | flops 5 | bytes 40 | tf_op jit(solution)/shard_map/psum | solution.py:172
  (735 shorter events, 467.8 us)
Async XLA Ops:
  56.6 5.7 collective-permute-start
  92.7 5.6 collective-permute-start.1
  114.0 54.0 %collective-permute-start.8 = (f32[3,4,1,256]{3,2,1,0:T(1,128)S(1)}, f32[3,4,1,256]{3,2,1,0:T(1,128)S(1)}, u32[]{:S(2)}, u32[]{:S(2)}) collective-permute-start(f32[3,4,1,256]{3,2,1,0:T(1,128)S(1)} %get-tuple-element.1741), channel_id=1, source_target_pairs={{0,4},{4,8},{8,12},{12,16},{16,20},{20,24},{24,28},{1,5},{5,9},{9,... | collective-permute-start | bytes 36872 | tf_op jit(solution)/shard_map/ppermute | solution.py:22
  116.7 51.2 %collective-permute-start.9 = (f32[3,4,1,256]{3,2,1,0:T(1,128)S(1)}, f32[3,4,1,256]{3,2,1,0:T(1,128)S(1)}, u32[]{:S(2)}, u32[]{:S(2)}) collective-permute-start(f32[3,4,1,256]{3,2,1,0:T(1,128)S(1)} %get-tuple-element.1742), channel_id=1, source_target_pairs={{4,0},{8,4},{12,8},{16,12},{20,16},{24,20},{28,24},{5,1},{9,5},{13... | collective-permute-start | bytes 36872 | tf_op jit(solution)/shard_map/ppermute | solution.py:25
  137.7 60.2 %all-to-all-start = ((s32[1,8,1024]{2,0,1:T(1,128)}), s32[1,8,1024]{2,0,1:T(1,128)S(1)}, u32[]{:S(2)}, u32[]{:S(2)}) async-start(s32[1,8,1024]{2,0,1:T(1,128)} %bitcast.141), calls=%async_computation | async-start | bytes 65536 | tf_op jit(solution)/shard_map/all_to_all | solution.py:139
  168.0 26.6 %collective-permute-start.10 = (f32[3,1,10,256]{3,2,1,0:T(8,128)S(1)}, f32[3,1,10,256]{3,2,1,0:T(8,128)S(1)}, u32[]{:S(2)}, u32[]{:S(2)}) collective-permute-start(f32[3,1,10,256]{3,2,1,0:T(8,128)S(1)} %get-tuple-element.1726), channel_id=1, source_target_pairs={{0,1},{1,2},{2,3},{4,5},{5,6},{6,7},{8,9},{9,10},{10,11},{12,13},{... | collective-permute-start | bytes 92168 | tf_op jit(solution)/shard_map/ppermute | solution.py:22
  171.5 23.1 %collective-permute-start.11 = (f32[3,1,10,256]{3,2,1,0:T(8,128)S(1)}, f32[3,1,10,256]{3,2,1,0:T(8,128)S(1)}, u32[]{:S(2)}, u32[]{:S(2)}) collective-permute-start(f32[3,1,10,256]{3,2,1,0:T(8,128)S(1)} %get-tuple-element.1725), channel_id=1, source_target_pairs={{1,0},{2,1},{3,2},{5,4},{6,5},{7,6},{9,8},{10,9},{11,10},{13,12},{... | collective-permute-start | bytes 92168 | tf_op jit(solution)/shard_map/ppermute | solution.py:25
  197.8 13.5 %all-to-all-start.1 = ((f32[3,8,1024]{2,0,1:T(4,128)}), f32[3,8,1024]{2,0,1:T(4,128)S(1)}, u32[]{:S(2)}, u32[]{:S(2)}) async-start(f32[3,8,1024]{2,0,1:T(4,128)} %copy.147), calls=%async_computation.1 | async-start | bytes 262144 | tf_op jit(solution)/shard_map/all_to_all | solution.py:165
  306.4 5.7 collective-permute-start.2
  354.5 24.6 %collective-permute-start.12 = (f32[3,4,1,256]{3,2,1,0:T(1,128)S(1)}, f32[3,4,1,256]{3,2,1,0:T(1,128)S(1)}, u32[]{:S(2)}, u32[]{:S(2)}) collective-permute-start(f32[3,4,1,256]{3,2,1,0:T(1,128)S(1)} %get-tuple-element.1739), channel_id=1, source_target_pairs={{0,4},{4,8},{8,12},{12,16},{16,20},{20,24},{24,28},{1,5},{5,9},{9,... | collective-permute-start | bytes 36872 | tf_op jit(solution)/shard_map/ppermute | solution.py:22
  356.7 22.4 %collective-permute-start.13 = (f32[3,4,1,256]{3,2,1,0:T(1,128)S(1)}, f32[3,4,1,256]{3,2,1,0:T(1,128)S(1)}, u32[]{:S(2)}, u32[]{:S(2)}) collective-permute-start(f32[3,4,1,256]{3,2,1,0:T(1,128)S(1)} %get-tuple-element.1740), channel_id=1, source_target_pairs={{4,0},{8,4},{12,8},{16,12},{20,16},{24,20},{28,24},{5,1},{9,5},{13... | collective-permute-start | bytes 36872 | tf_op jit(solution)/shard_map/ppermute | solution.py:25
  379.1 28.4 %collective-permute-start.14 = (f32[3,1,10,256]{3,2,1,0:T(8,128)S(1)}, f32[3,1,10,256]{3,2,1,0:T(8,128)S(1)}, u32[]{:S(2)}, u32[]{:S(2)}) collective-permute-start(f32[3,1,10,256]{3,2,1,0:T(8,128)S(1)} %get-tuple-element.1722), channel_id=1, source_target_pairs={{0,1},{1,2},{2,3},{4,5},{5,6},{6,7},{8,9},{9,10},{10,11},{12,13},{... | collective-permute-start | bytes 92168 | tf_op jit(solution)/shard_map/ppermute | solution.py:22
  383.2 24.4 %collective-permute-start.15 = (f32[3,1,10,256]{3,2,1,0:T(8,128)S(1)}, f32[3,1,10,256]{3,2,1,0:T(8,128)S(1)}, u32[]{:S(2)}, u32[]{:S(2)}) collective-permute-start(f32[3,1,10,256]{3,2,1,0:T(8,128)S(1)} %get-tuple-element.1721), channel_id=1, source_target_pairs={{1,0},{2,1},{3,2},{5,4},{6,5},{7,6},{9,8},{10,9},{11,10},{13,12},{... | collective-permute-start | bytes 92168 | tf_op jit(solution)/shard_map/ppermute | solution.py:25
  403.2 11.9 %all-to-all-start.2 = ((f32[3,8,1024]{2,0,1:T(4,128)}), f32[3,8,1024]{2,0,1:T(4,128)S(1)}, u32[]{:S(2)}, u32[]{:S(2)}) async-start(f32[3,8,1024]{2,0,1:T(4,128)} %copy.156), calls=%async_computation.2 | async-start | bytes 262144 | tf_op jit(solution)/shard_map/all_to_all | solution.py:165
  511.6 5.7 collective-permute-start.4
  580.8 25.8 %collective-permute-start.16 = (f32[3,4,1,256]{3,2,1,0:T(1,128)S(1)}, f32[3,4,1,256]{3,2,1,0:T(1,128)S(1)}, u32[]{:S(2)}, u32[]{:S(2)}) collective-permute-start(f32[3,4,1,256]{3,2,1,0:T(1,128)S(1)} %get-tuple-element.1737), channel_id=1, source_target_pairs={{0,4},{4,8},{8,12},{12,16},{16,20},{20,24},{24,28},{1,5},{5,9},{9,... | collective-permute-start | bytes 36872 | tf_op jit(solution)/shard_map/ppermute | solution.py:22
  582.5 24.0 %collective-permute-start.17 = (f32[3,4,1,256]{3,2,1,0:T(1,128)S(1)}, f32[3,4,1,256]{3,2,1,0:T(1,128)S(1)}, u32[]{:S(2)}, u32[]{:S(2)}) collective-permute-start(f32[3,4,1,256]{3,2,1,0:T(1,128)S(1)} %get-tuple-element.1738), channel_id=1, source_target_pairs={{4,0},{8,4},{12,8},{16,12},{20,16},{24,20},{28,24},{5,1},{9,5},{13... | collective-permute-start | bytes 36872 | tf_op jit(solution)/shard_map/ppermute | solution.py:25
  602.7 15.6 %all-to-all-start.3 = ((f32[3,8,1024]{2,0,1:T(4,128)}), f32[3,8,1024]{2,0,1:T(4,128)S(1)}, u32[]{:S(2)}, u32[]{:S(2)}) async-start(f32[3,8,1024]{2,0,1:T(4,128)} %copy.165), calls=%async_computation.3 | async-start | bytes 262144 | tf_op jit(solution)/shard_map/all_to_all | solution.py:165
  606.6 8.3 collective-permute-start.18
  720.6 5.7 collective-permute-start.6
  789.7 25.7 %collective-permute-start.20 = (f32[3,4,1,256]{3,2,1,0:T(1,128)S(1)}, f32[3,4,1,256]{3,2,1,0:T(1,128)S(1)}, u32[]{:S(2)}, u32[]{:S(2)}) collective-permute-start(f32[3,4,1,256]{3,2,1,0:T(1,128)S(1)} %get-tuple-element.1735), channel_id=1, source_target_pairs={{0,4},{4,8},{8,12},{12,16},{16,20},{20,24},{24,28},{1,5},{5,9},{9,... | collective-permute-start | bytes 36872 | tf_op jit(solution)/shard_map/ppermute | solution.py:22
  791.0 24.4 %collective-permute-start.21 = (f32[3,4,1,256]{3,2,1,0:T(1,128)S(1)}, f32[3,4,1,256]{3,2,1,0:T(1,128)S(1)}, u32[]{:S(2)}, u32[]{:S(2)}) collective-permute-start(f32[3,4,1,256]{3,2,1,0:T(1,128)S(1)} %get-tuple-element.1736), channel_id=1, source_target_pairs={{4,0},{8,4},{12,8},{16,12},{20,16},{24,20},{28,24},{5,1},{9,5},{13... | collective-permute-start | bytes 36872 | tf_op jit(solution)/shard_map/ppermute | solution.py:25
  811.2 16.0 %all-to-all-start.4 = ((f32[3,8,1024]{2,0,1:T(4,128)}), f32[3,8,1024]{2,0,1:T(4,128)S(1)}, u32[]{:S(2)}, u32[]{:S(2)}) async-start(f32[3,8,1024]{2,0,1:T(4,128)} %copy.174), calls=%async_computation.4 | async-start | bytes 262144 | tf_op jit(solution)/shard_map/all_to_all | solution.py:165
  815.5 8.3 collective-permute-start.22
  (52 other events, 1136.3 us)
